TPU v7x, 256 devices: a whole 4x4x8 slice. The times are simulated.
256 devices in a mesh: row: 8 (over y, core), col: 32 (over x, z).
Axes of the slice: x: 4, y: 4, z: 8, core: 2. Of those that a mesh axis runs over, the one named last changes fastest.
Arguments:
- features: bfloat16 [65536, 512], P(('row', 'col')), may hold values from -6 to 6
- memory: float32 [65536, 512], P(('col', 'row')), may hold values from -1 to 1
- tile_values: bfloat16 [8, 32, 128, 128, 128], P('row', 'col'), as said below
- tile_rows: int32 [8, 32, 128], P('row', 'col'), may hold values from 0 to 15, as said below
- tile_cols: int32 [8, 32, 128], P('row', 'col'), may hold values from 0 to 63
- tile_count: int32 [8, 32], P('row', 'col'), may hold values from 16 to 128, as said below
- conv_weight: bfloat16 [512, 512], replicated, may hold values from -0.25 to 0.25
- conv_bias: float32 [512], replicated, may hold values from -3 to 3
- input_weight: bfloat16 [512, 1536], replicated, may hold values from -0.25 to 0.25
- input_bias: float32 [1536], replicated, may hold values from -3 to 3
- hidden_weight: bfloat16 [512, 1536], replicated, may hold values from -0.25 to 0.25
- hidden_bias: float32 [1536], replicated, may hold values from -3 to 3
Outputs:
- new_memory: float32 [65536, 512], P(('col', 'row'))
Inputs may be any that keep to these rules, and one draw needn't show every extreme that they name: `tile_values`: edge weights are nonnegative. For each device pair (r, c) the 128 pairs (tile_rows, tile_cols) are distinct. `tile_count`: in every draw some device pair has all 128 slots live.
All inputs are finite; a program needn't handle non-finite values.
Results may differ from a plain program's by a relative error of at most 0.017.
Values may be sent and summed in bfloat16 or wider, within the bound.
A program may use at most 128 MiB of HBM per device.

v0:
```python
import jax
import jax.numpy as jnp
from jax import lax
from jax.sharding import PartitionSpec as P

norm_epsilon = 1e-06
tiles_per_pass = 32


def gru_update(message, memory, input_weight, input_bias, hidden_weight, hidden_bias):
    width = memory.shape[1]
    from_input = jnp.dot(message, input_weight, preferred_element_type=jnp.float32) + input_bias
    held = memory.astype(jnp.bfloat16)
    from_memory = jnp.dot(held, hidden_weight, preferred_element_type=jnp.float32) + hidden_bias
    reset = jax.nn.sigmoid(from_input[:, :width] + from_memory[:, :width])
    update = jax.nn.sigmoid(from_input[:, width : 2 * width] + from_memory[:, width : 2 * width])
    candidate = jnp.tanh(from_input[:, 2 * width :] + reset * from_memory[:, 2 * width :])
    return (1.0 - update) * candidate + update * memory


def on_device(
    features,
    memory,
    tile_values,
    tile_rows,
    tile_cols,
    tile_count,
    conv_weight,
    conv_bias,
    input_weight,
    input_bias,
    hidden_weight,
    hidden_bias,
):
    own_rows, width = features.shape
    tile_data = tile_values[0, 0]
    row_ids = tile_rows[0, 0]
    col_ids = tile_cols[0, 0]
    live_count = tile_count[0, 0]
    slot_total = tile_data.shape[0]
    tile_size = tile_data.shape[1]
    row_blocks = own_rows * lax.axis_size("row") // tile_size
    col_blocks = own_rows * lax.axis_size("col") // tile_size
    per_pass = min(tiles_per_pass, slot_total)
    live = jnp.arange(slot_total) < live_count
    column_sums = jnp.sum(tile_data, axis=1, dtype=jnp.float32) * live[:, None]
    picker = ((col_ids[:, None] == jnp.arange(col_blocks)[None, :]) & live[:, None]).astype(
        jnp.float32
    )
    out_terms = jnp.einsum(
        "tb,tq->bq", picker, column_sums, precision=lax.Precision.HIGHEST
    ).reshape(col_blocks * tile_size)
    gathered = lax.all_gather(features, "col", axis=0, tiled=True)
    all_degree = 1.0 + lax.psum(out_terms.astype(jnp.bfloat16), "col").astype(jnp.float32)
    gathered = (gathered.astype(jnp.float32) * lax.rsqrt(all_degree)[:, None]).astype(jnp.bfloat16)
    panel = gathered.reshape(col_blocks, tile_size, width)

    def advance(block_index, summed):
        first_slot = block_index * per_pass
        block_rows = lax.dynamic_slice_in_dim(row_ids, first_slot, per_pass)
        block_cols = lax.dynamic_slice_in_dim(col_ids, first_slot, per_pass)
        block_tiles = lax.dynamic_slice_in_dim(tile_data, first_slot, per_pass)
        block_live = first_slot + jnp.arange(per_pass) < live_count
        block_tiles = jnp.where(block_live[:, None, None], block_tiles, jnp.zeros((), jnp.bfloat16))
        picked = jnp.take(panel, block_cols, axis=0)
        products = jnp.einsum(
            "tpq,tqf->tpf", block_tiles, picked, preferred_element_type=jnp.float32
        )
        return summed.at[block_rows].add(products)

    passes = (live_count + per_pass - 1) // per_pass
    summed = lax.fori_loop(
        0, passes, advance, jnp.zeros((row_blocks, tile_size, width), jnp.float32)
    )
    partial_value = summed.reshape(row_blocks * tile_size, width)
    owned = lax.psum_scatter(
        partial_value.astype(jnp.bfloat16), "row", scatter_dimension=0, tiled=True
    ).astype(jnp.float32)
    normed = (
        owned / jnp.sqrt(jnp.mean(owned * owned, axis=1, keepdims=True) + norm_epsilon)
    ).astype(jnp.bfloat16)
    message = jax.nn.relu(
        jnp.dot(normed, conv_weight, preferred_element_type=jnp.float32) + conv_bias
    ).astype(jnp.bfloat16)
    return gru_update(message, memory, input_weight, input_bias, hidden_weight, hidden_bias)


def solution(mesh):
    placed = (
        P(("row", "col"), None),
        P(("col", "row"), None),
        P("row", "col", None, None, None),
        P("row", "col", None),
        P("row", "col", None),
        P("row", "col"),
        P(),
        P(),
        P(),
        P(),
        P(),
        P(),
    )
    return jax.shard_map(
        on_device, mesh=mesh, in_specs=placed, out_specs=P(("col", "row"), None), check_vma=False
    )
```

profile of v0, /device:TPU:4, one launch (start us, length us, event | category | flops | bytes accessed | tf_op | source)
XLA Modules:
  0.0 344.7 jit_solution(16640008878866599915)
XLA Ops:
  6.5 0.0 copy-start
  6.5 0.0 copy-start.1
  6.5 0.0 all-gather.2.cloned.1.call-start
  6.5 0.7 all-gather.2.cloned.1.call-update
  7.3 0.0 reduce-scatter.2.cloned.1.call-start
  8.0 3.4 convert_reduce_fusion
  11.4 0.0 copy-done.1
  11.4 0.3 fusion.13
  11.7 125.3 %psum.7 = bf16[8192]{0:T(1024)(128)(2,1)S(1)} all-reduce(bf16[8192]{0:T(1024)(128)(2,1)S(1)} %fusion.13), channel_id=1, replica_groups=mesh['row'=8,'col'=32] {'col'}, use_global_device_ids=true, to_apply=%region_1.0 | all-reduce | flops 8192 | bytes 32768 | tf_op jit(solution)/shard_map/psum | solution.py:54
  137.0 0.0 all-gather.2.cloned.1.call-done
  137.1 7.6 %multiply_convert_fusion = bf16[8192,512]{1,0:T(8,128)(2,1)} fusion(bf16[8192,512]{1,0:T(8,128)(2,1)} %all-gather.2.cloned.1.call-done, f32[8192]{0:T(1024)S(1)} %add_rsqrt_fusion), kind=kLoop, calls=%fused_computation.18 | loop fusion | flops 12582912 | bytes 16809984 | tf_op jit(solution)/shard_map/convert_element_type | solution.py:55
  144.7 0.0 copy-start.5
  144.7 2.5 broadcast_in_dim.39
  147.2 0.0 copy-done.5
  147.2 129.4 %while.10 = (s32[]{:T(128)}, f32[16,128,512]{2,1,0:T(8,128)}, s32[]{:T(128)}, s32[128]{0:T(128)S(1)}, s32[]{:T(128)}, /*index=5*/bf16[128,128,128]{2,1,0:T(8,128...) while((s32[]{:T(128)}, f32[16,128,512]{2,1,0:T(8,128)}, ...), condition=%wide.region_4.5_spmd, body=%wide.region_2.4_spmd.sunk | while | flops 541590912 | bytes 47191224 | solution.py:72
  147.2 0.7 compare_and_fusion.2
  147.9 6.1 %gather_fusion = bf16[32,128,512]{2,1,0:T(8,128)(2,1)} fusion(bf16[64,128,512]{2,1,0:T(8,128)(2,1)} %get-tuple-element.157, s32[1024]{0:T(1024)S(1)} %pad_clamp_fusion.2), kind=kCustom, calls=%fused_computation.clone.1 | custom fusion | bytes 8388736 | tf_op jit(solution)/shard_map/while/body/jit(_take)/gather | solution.py:65
  154.1 7.0 %fusion.51 = f32[32,128,512]{2,1,0:T(8,128)} fusion(bf16[32,128,512]{2,1,0:T(8,128)(2,1)} %gather_fusion, pred[32]{0:T(512)(128)(4,1)S(1)} %get-tuple-element.124, bf16[128,128,128]{2,1,0:T(8,128)(2,1)} %get-tuple-element.155, s32[]{:T(128)S(6)} %select_n.41, pred[32]{0:T(512)(128)(4,1)S(1)} %get-tuple-element.125), kind=kOutput, calls=%fused_computation.2.clone.1 | convolution fusion | flops 539492352 | bytes 13631556 | tf_op jit(solution)/shard_map/while/body/tpq,tqf->tpf/dot_general | solution.py:66
  161.1 0.1 compare_select_fusion.4
  161.2 18.2 %scatter_fusion = f32[16,128,512]{2,1,0:T(8,128)} fusion(f32[16,128,512]{2,1,0:T(8,128)} %get-tuple-element.139, s32[32]{0:T(128)S(1)} %compare_select_fusion.4, f32[32,128,512]{2,1,0:T(8,128)} %fusion.51), kind=kCustom, calls=%fused_computation.1.clone.1 | custom fusion | flops 2097152 | bytes 25165952 | tf_op jit(solution)/shard_map/while/body/scatter-add | solution.py:69
  179.4 0.7 compare_and_fusion.2
  180.1 6.1 %gather_fusion = bf16[32,128,512]{2,1,0:T(8,128)(2,1)} fusion(bf16[64,128,512]{2,1,0:T(8,128)(2,1)} %get-tuple-element.157, s32[1024]{0:T(1024)S(1)} %pad_clamp_fusion.2), kind=kCustom, calls=%fused_computation.clone.1 | custom fusion | bytes 8388736 | tf_op jit(solution)/shard_map/while/body/jit(_take)/gather | solution.py:65
  186.2 7.0 %fusion.51 = f32[32,128,512]{2,1,0:T(8,128)} fusion(bf16[32,128,512]{2,1,0:T(8,128)(2,1)} %gather_fusion, pred[32]{0:T(512)(128)(4,1)S(1)} %get-tuple-element.124, bf16[128,128,128]{2,1,0:T(8,128)(2,1)} %get-tuple-element.155, s32[]{:T(128)S(6)} %select_n.41, pred[32]{0:T(512)(128)(4,1)S(1)} %get-tuple-element.125), kind=kOutput, calls=%fused_computation.2.clone.1 | convolution fusion | flops 539492352 | bytes 13631556 | tf_op jit(solution)/shard_map/while/body/tpq,tqf->tpf/dot_general | solution.py:66
  193.3 0.1 compare_select_fusion.4
  193.4 18.4 %scatter_fusion = f32[16,128,512]{2,1,0:T(8,128)} fusion(f32[16,128,512]{2,1,0:T(8,128)} %get-tuple-element.139, s32[32]{0:T(128)S(1)} %compare_select_fusion.4, f32[32,128,512]{2,1,0:T(8,128)} %fusion.51), kind=kCustom, calls=%fused_computation.1.clone.1 | custom fusion | flops 2097152 | bytes 25165952 | tf_op jit(solution)/shard_map/while/body/scatter-add | solution.py:69
  211.8 0.7 compare_and_fusion.2
  212.5 6.1 %gather_fusion = bf16[32,128,512]{2,1,0:T(8,128)(2,1)} fusion(bf16[64,128,512]{2,1,0:T(8,128)(2,1)} %get-tuple-element.157, s32[1024]{0:T(1024)S(1)} %pad_clamp_fusion.2), kind=kCustom, calls=%fused_computation.clone.1 | custom fusion | bytes 8388736 | tf_op jit(solution)/shard_map/while/body/jit(_take)/gather | solution.py:65
  218.6 7.0 %fusion.51 = f32[32,128,512]{2,1,0:T(8,128)} fusion(bf16[32,128,512]{2,1,0:T(8,128)(2,1)} %gather_fusion, pred[32]{0:T(512)(128)(4,1)S(1)} %get-tuple-element.124, bf16[128,128,128]{2,1,0:T(8,128)(2,1)} %get-tuple-element.155, s32[]{:T(128)S(6)} %select_n.41, pred[32]{0:T(512)(128)(4,1)S(1)} %get-tuple-element.125), kind=kOutput, calls=%fused_computation.2.clone.1 | convolution fusion | flops 539492352 | bytes 13631556 | tf_op jit(solution)/shard_map/while/body/tpq,tqf->tpf/dot_general | solution.py:66
  225.7 0.1 compare_select_fusion.4
  225.7 18.5 %scatter_fusion = f32[16,128,512]{2,1,0:T(8,128)} fusion(f32[16,128,512]{2,1,0:T(8,128)} %get-tuple-element.139, s32[32]{0:T(128)S(1)} %compare_select_fusion.4, f32[32,128,512]{2,1,0:T(8,128)} %fusion.51), kind=kCustom, calls=%fused_computation.1.clone.1 | custom fusion | flops 2097152 | bytes 25165952 | tf_op jit(solution)/shard_map/while/body/scatter-add | solution.py:69
  244.2 0.7 compare_and_fusion.2
  244.9 6.1 %gather_fusion = bf16[32,128,512]{2,1,0:T(8,128)(2,1)} fusion(bf16[64,128,512]{2,1,0:T(8,128)(2,1)} %get-tuple-element.157, s32[1024]{0:T(1024)S(1)} %pad_clamp_fusion.2), kind=kCustom, calls=%fused_computation.clone.1 | custom fusion | bytes 8388736 | tf_op jit(solution)/shard_map/while/body/jit(_take)/gather | solution.py:65
  251.1 7.0 %fusion.51 = f32[32,128,512]{2,1,0:T(8,128)} fusion(bf16[32,128,512]{2,1,0:T(8,128)(2,1)} %gather_fusion, pred[32]{0:T(512)(128)(4,1)S(1)} %get-tuple-element.124, bf16[128,128,128]{2,1,0:T(8,128)(2,1)} %get-tuple-element.155, s32[]{:T(128)S(6)} %select_n.41, pred[32]{0:T(512)(128)(4,1)S(1)} %get-tuple-element.125), kind=kOutput, calls=%fused_computation.2.clone.1 | convolution fusion | flops 539492352 | bytes 13631556 | tf_op jit(solution)/shard_map/while/body/tpq,tqf->tpf/dot_general | solution.py:66
  258.1 0.1 compare_select_fusion.4
  258.2 18.4 %scatter_fusion = f32[16,128,512]{2,1,0:T(8,128)} fusion(f32[16,128,512]{2,1,0:T(8,128)} %get-tuple-element.139, s32[32]{0:T(128)S(1)} %compare_select_fusion.4, f32[32,128,512]{2,1,0:T(8,128)} %fusion.51), kind=kCustom, calls=%fused_computation.1.clone.1 | custom fusion | flops 2097152 | bytes 25165952 | tf_op jit(solution)/shard_map/while/body/scatter-add | solution.py:69
  276.6 0.0 copy-start.2
  276.6 3.8 %convert_element_type.52 = bf16[16,128,512]{2,1,0:T(8,128)(2,1)} convert(f32[16,128,512]{2,1,0:T(8,128)} %get-tuple-element.48) | non-fusion elementwise | flops 1048576 | bytes 6291456 | tf_op jit(solution)/shard_map/convert_element_type | solution.py:77
  280.4 0.0 copy-start.3
  280.4 0.0 reduce-scatter.2.cloned.1.call-update
  280.5 0.0 copy-done
  280.5 0.0 copy-done.2
  280.5 1.6 convolution_add_fusion
  282.1 48.2 %reduce-scatter.2.cloned.1.call-done = bf16[256,512]{1,0:T(8,128)(2,1)} async-done(((bf16[2048,512]{1,0:T(8,128)(2,1)}), bf16[256,512]{1,0:T(8,128)(2,1)}) %reduce-scatter.2.cloned.1.call-update) | async-done | bytes 262160 | tf_op jit(solution)/shard_map/reduce_scatter | solution.py:76
  330.3 1.1 fusion.14
  331.4 0.0 copy-done.3
  331.4 0.0 copy-done.4
  331.5 3.7 %convolution_add_fusion.1 = f32[256,1536]{1,0:T(8,128)} fusion(bf16[512,1536]{1,0:T(8,128)(2,1)} %param.22, bf16[512,512]{1,0:T(8,128)(2,1)} %param.20, f32[1536]{0:T(1024)S(1)} %copy-done.3, bf16[256,512]{1,0:T(8,128)(2,1)} %reduce-scatter.2.cloned.1.call-done, f32[512]{0:T(512)S(1)} %copy-done.4, f32[256]{0:T(256)S(1)} %add_sqrt_fusion), kind=kOutput, calls=%fused_computation.21 | convolution fusion | flops 538050560 | bytes 3941376 | tf_op jit(solution)/shard_map/dot_general | solution.py:12
  335.1 2.8 fusion.19
  (8 shorter events, 0.1 us)
Async XLA Ops:
  6.5 273.9 %copy-start = (bf16[512,1536]{1,0:T(8,128)(2,1)S(1)}, bf16[512,1536]{1,0:T(8,128)(2,1)}, u32[]{:S(2)}) copy-start(bf16[512,1536]{1,0:T(8,128)(2,1)} %param.24) | copy-start | bytes 4718596
  6.5 4.9 %copy-start.1 = (s32[1,1,128]{2,1,0:T(1,128)S(1)}, s32[1,1,128]{2,1,0:T(1,128)}, u32[]{:S(2)}) copy-start(s32[1,1,128]{2,1,0:T(1,128)} %param.18) | copy-start | bytes 1540
  6.5 130.5 %all-gather.2.cloned.1.call-start = ((), (), s32[]{:S(2)}) async-start(), calls=%async_computation.1 | async-start | bytes 8650752 | tf_op jit(solution)/shard_map/all_gather | solution.py:53
  7.3 323.1 %reduce-scatter.2.cloned.1.call-start = ((), (), s32[]{:S(2)}) async-start(), calls=%async_computation.2 | async-start | bytes 2359296 | tf_op jit(solution)/shard_map/reduce_scatter | solution.py:76
  144.7 2.5 copy-start.5
  276.6 3.9 %copy-start.2 = (f32[1536]{0:T(1024)S(1)}, f32[1536]{0:T(1024)}, u32[]{:S(2)}) copy-start(f32[1536]{0:T(1024)} %param.25) | copy-start | bytes 18436
  280.4 51.0 %copy-start.3 = (f32[1536]{0:T(1024)S(1)}, f32[1536]{0:T(1024)}, u32[]{:S(2)}) copy-start(f32[1536]{0:T(1024)} %param.23) | copy-start | bytes 18436
  280.4 51.0 %copy-start.4 = (f32[512]{0:T(512)S(1)}, f32[512]{0:T(512)}, u32[]{:S(2)}) copy-start(f32[512]{0:T(512)} %param.21) | copy-start | bytes 6148
Sparse Core Ops, SparseCore 0:
  10.0 100.8 all-gather.1
  280.6 49.7 reduce-scatter.1
where the time goes:
time: 345 us
  blocking collectives  125 us (36%)
  other arithmetic  95.5 us (28%)
  waiting for transfers between devices  49 us (14%)
  matrix products  33.7 us (10%)
  local copies, waits for them, and re-layouts  27.1 us (8%)
  between operations  14.2 us (4%)
    psum x1, blocking collectives, on_device(): lax.psum(out_terms.astype(jnp.bfloat16), 'col').astype(jnp.float32)  125 us
    scatter-add x4, other arithmetic, advance(): return summed.at[block_rows].add(products)  73.5 us
    reduce_scatter x1, waiting for transfers between devices, on_device(): lax.psum_scatter(partial_value.astype(jnp.bfloat16), 'row', scatter_dimen...  48.2 us
    dot_general x4, matrix products, advance(): jnp.einsum('tpq,tqf->tpf', block_tiles, picked, preferred_element_type=jn...  28.1 us
    gather x4, local copies, waits for them, and re-layouts, advance(): picked = jnp.take(panel, block_cols, axis=0)  24.5 us
    convert_element_type x1, other arithmetic, on_device(): (gathered.astype(jnp.float32) * lax.rsqrt(all_degree)[:, None]).astype(jn...  7.63 us
  transfers between devices with their start and end apart: 2, of which 1 were waited for; matrix products, arithmetic and copies ran while one was open for 2% of the time, Pallas kernels for 0%

commit v1 on v0

--- a/solution.py
+++ b/solution.py
@@ -2,9 +2,15 @@
 import jax.numpy as jnp
 from jax import lax
 from jax.sharding import PartitionSpec as P
+from jax.lax import all_gather
 
 norm_epsilon = 1e-06
 tiles_per_pass = 32
+
+
+def advance_runs(inner_x, mesh_ax):
+    b_now = jnp.sum(all_gather(inner_x, axis_name=mesh_ax), 0)
+    return b_now
 
 
 def gru_update(message, memory, input_weight, input_bias, hidden_weight, hidden_bias):
@@ -51,7 +57,7 @@
         "tb,tq->bq", picker, column_sums, precision=lax.Precision.HIGHEST
     ).reshape(col_blocks * tile_size)
     gathered = lax.all_gather(features, "col", axis=0, tiled=True)
-    all_degree = 1.0 + lax.psum(out_terms.astype(jnp.bfloat16), "col").astype(jnp.float32)
+    all_degree = 1.0 + advance_runs(out_terms.astype(jnp.bfloat16), "col").astype(jnp.float32)
     gathered = (gathered.astype(jnp.float32) * lax.rsqrt(all_degree)[:, None]).astype(jnp.bfloat16)
     panel = gathered.reshape(col_blocks, tile_size, width)
 

time: 345 us -> 303 us (0.88)
  blocking collectives: 125 us -> 53.2 us
  waiting for transfers between devices: 49 us -> 77.1 us
    psum x1 -> x0, blocking collectives: 125 us -> none  [on_device(): lax.psum(out_terms.astype(jnp.bfloat16), 'col').astype(jnp.float32)]
    all_gather x0 -> x1, blocking collectives: none -> 53.2 us  [advance_runs(): b_now = jnp.sum(all_gather(inner_x, axis_name=mesh_ax), 0)]
    all_gather x1, waiting for transfers between devices: 0.02 us -> 44.2 us  [on_device(): gathered = lax.all_gather(features, 'col', axis=0, tiled=True)]
    reduce_scatter x1, waiting for transfers between devices: 48.2 us -> 32.1 us  [on_device(): lax.psum_scatter(partial_value.astype(jnp.bfloat16), 'row', scatter_dimen...]
  transfers between devices with their start and end apart: 2 -> 2, of which waited for: 1 -> 2; matrix products, arithmetic and copies ran while one was open for 2% -> 2% of each run, Pallas kernels for 0% -> 0%
where the time goes in v1:
time: 303 us; the launch traced here: 302 us
  other arithmetic  96.4 us (32%)
  waiting for transfers between devices  77.1 us (25%)
  blocking collectives  53.2 us (18%)
  matrix products  33.7 us (11%)
  local copies, waits for them, and re-layouts  27.1 us (9%)
  between operations  14.2 us (5%)
    scatter-add x4, other arithmetic, advance(): return summed.at[block_rows].add(products)  73.5 us
    all_gather x1, blocking collectives, advance_runs(): b_now = jnp.sum(all_gather(inner_x, axis_name=mesh_ax), 0)  53.2 us
    all_gather x1, waiting for transfers between devices, on_device(): gathered = lax.all_gather(features, 'col', axis=0, tiled=True)  44.2 us
    reduce_scatter x1, waiting for transfers between devices, on_device(): lax.psum_scatter(partial_value.astype(jnp.bfloat16), 'row', scatter_dimen...  32.1 us
    dot_general x4, matrix products, advance(): jnp.einsum('tpq,tqf->tpf', block_tiles, picked, preferred_element_type=jn...  28.1 us
    gather x4, local copies, waits for them, and re-layouts, advance(): picked = jnp.take(panel, block_cols, axis=0)  24.5 us
    convert_element_type x1, other arithmetic, on_device(): (gathered.astype(jnp.float32) * lax.rsqrt(all_degree)[:, None]).astype(jn...  7.63 us
  transfers between devices with their start and end apart: 2, of which 2 were waited for; matrix products, arithmetic and copies ran while one was open for 2% of the time, Pallas kernels for 0%

profile of v1, /device:TPU:4, one launch (start us, length us, event | category | flops | bytes accessed | tf_op | source)
XLA Modules:
  0.0 301.8 jit_solution(13938603511683014078)
XLA Ops:
  6.5 0.0 copy-start
  6.5 0.0 copy-start.1
  6.5 0.0 all-gather.3.cloned.1.call-start
  6.5 0.7 all-gather.3.cloned.1.call-update
  7.3 0.0 reduce-scatter.2.cloned.1.call-start
  8.0 3.4 %convert_reduce_fusion = f32[128,128]{1,0:T(8,128)S(1)} fusion(bf16[1,1,128,128,128]{4,3,2,1,0:T(8,128)(2,1)} %param.16), kind=kLoop, calls=%fused_computation.19 | loop fusion | flops 4177920 | bytes 4259840 | tf_op jit(solution)/shard_map/reduce_sum | solution.py:52
  11.4 0.0 copy-done.1
  11.4 0.3 convolution_convert_fusion
  11.8 53.2 %all-gather = bf16[32,1,8192]{2,1,0:T(2,128)(2,1)S(1)} all-gather(bf16[1,1,8192]{2,1,0:T(2,128)(2,1)S(1)} %reshape.71), channel_id=1, replica_groups=mesh['row'=8,'col'=32] {'col'}, dimensions={0}, use_global_device_ids=true | all-gather | bytes 540672 | tf_op jit(solution)/shard_map/all_gather | solution.py:12
  65.0 1.0 reduce_sum.31
  66.0 44.2 %all-gather.3.cloned.1.call-done = bf16[8192,512]{1,0:T(8,128)(2,1)} async-done(((bf16[256,512]{1,0:T(8,128)(2,1)}), bf16[8192,512]{1,0:T(8,128)(2,1)}) %all-gather.3.cloned.1.call-update) | async-done | bytes 8388624 | tf_op jit(solution)/shard_map/all_gather | solution.py:59
  110.3 7.6 %multiply_convert_fusion = bf16[8192,512]{1,0:T(8,128)(2,1)} fusion(bf16[8192,512]{1,0:T(8,128)(2,1)} %all-gather.3.cloned.1.call-done, f32[8192]{0:T(1024)S(1)} %add_rsqrt_fusion), kind=kLoop, calls=%fused_computation.18 | loop fusion | flops 12582912 | bytes 16809984 | tf_op jit(solution)/shard_map/convert_element_type | solution.py:61
  117.9 0.0 copy-start.5
  117.9 2.5 broadcast_in_dim.39
  120.4 0.0 copy-done.5
  120.4 129.4 %while.10 = (s32[]{:T(128)}, f32[16,128,512]{2,1,0:T(8,128)}, s32[]{:T(128)}, s32[128]{0:T(128)S(1)}, s32[]{:T(128)}, /*index=5*/bf16[128,128,128]{2,1,0:T(8,128...) while((s32[]{:T(128)}, f32[16,128,512]{2,1,0:T(8,128)}, ...), condition=%wide.region_4.5_spmd, body=%wide.region_2.4_spmd.sunk | while | flops 541590912 | bytes 47191224 | solution.py:78
  120.4 0.7 compare_and_fusion.2
  121.1 6.1 %gather_fusion = bf16[32,128,512]{2,1,0:T(8,128)(2,1)} fusion(bf16[64,128,512]{2,1,0:T(8,128)(2,1)} %get-tuple-element.157, s32[1024]{0:T(1024)S(1)} %pad_clamp_fusion.2), kind=kCustom, calls=%fused_computation.clone.1 | custom fusion | bytes 8388736 | tf_op jit(solution)/shard_map/while/body/jit(_take)/gather | solution.py:71
  127.3 7.0 %fusion.50 = f32[32,128,512]{2,1,0:T(8,128)} fusion(bf16[32,128,512]{2,1,0:T(8,128)(2,1)} %gather_fusion, pred[32]{0:T(512)(128)(4,1)S(1)} %get-tuple-element.124, bf16[128,128,128]{2,1,0:T(8,128)(2,1)} %get-tuple-element.155, s32[]{:T(128)S(6)} %select_n.41, pred[32]{0:T(512)(128)(4,1)S(1)} %get-tuple-element.125), kind=kOutput, calls=%fused_computation.2.clone.1 | convolution fusion | flops 539492352 | bytes 13631556 | tf_op jit(solution)/shard_map/while/body/tpq,tqf->tpf/dot_general | solution.py:72
  134.3 0.1 compare_select_fusion.4
  134.4 18.2 %scatter_fusion = f32[16,128,512]{2,1,0:T(8,128)} fusion(f32[16,128,512]{2,1,0:T(8,128)} %get-tuple-element.139, s32[32]{0:T(128)S(1)} %compare_select_fusion.4, f32[32,128,512]{2,1,0:T(8,128)} %fusion.50), kind=kCustom, calls=%fused_computation.1.clone.1 | custom fusion | flops 2097152 | bytes 25165952 | tf_op jit(solution)/shard_map/while/body/scatter-add | solution.py:75
  152.6 0.7 compare_and_fusion.2
  153.3 6.1 %gather_fusion = bf16[32,128,512]{2,1,0:T(8,128)(2,1)} fusion(bf16[64,128,512]{2,1,0:T(8,128)(2,1)} %get-tuple-element.157, s32[1024]{0:T(1024)S(1)} %pad_clamp_fusion.2), kind=kCustom, calls=%fused_computation.clone.1 | custom fusion | bytes 8388736 | tf_op jit(solution)/shard_map/while/body/jit(_take)/gather | solution.py:71
  159.4 7.0 %fusion.50 = f32[32,128,512]{2,1,0:T(8,128)} fusion(bf16[32,128,512]{2,1,0:T(8,128)(2,1)} %gather_fusion, pred[32]{0:T(512)(128)(4,1)S(1)} %get-tuple-element.124, bf16[128,128,128]{2,1,0:T(8,128)(2,1)} %get-tuple-element.155, s32[]{:T(128)S(6)} %select_n.41, pred[32]{0:T(512)(128)(4,1)S(1)} %get-tuple-element.125), kind=kOutput, calls=%fused_computation.2.clone.1 | convolution fusion | flops 539492352 | bytes 13631556 | tf_op jit(solution)/shard_map/while/body/tpq,tqf->tpf/dot_general | solution.py:72
  166.5 0.1 compare_select_fusion.4
  166.6 18.4 %scatter_fusion = f32[16,128,512]{2,1,0:T(8,128)} fusion(f32[16,128,512]{2,1,0:T(8,128)} %get-tuple-element.139, s32[32]{0:T(128)S(1)} %compare_select_fusion.4, f32[32,128,512]{2,1,0:T(8,128)} %fusion.50), kind=kCustom, calls=%fused_computation.1.clone.1 | custom fusion | flops 2097152 | bytes 25165952 | tf_op jit(solution)/shard_map/while/body/scatter-add | solution.py:75
  185.0 0.7 compare_and_fusion.2
  185.7 6.1 %gather_fusion = bf16[32,128,512]{2,1,0:T(8,128)(2,1)} fusion(bf16[64,128,512]{2,1,0:T(8,128)(2,1)} %get-tuple-element.157, s32[1024]{0:T(1024)S(1)} %pad_clamp_fusion.2), kind=kCustom, calls=%fused_computation.clone.1 | custom fusion | bytes 8388736 | tf_op jit(solution)/shard_map/while/body/jit(_take)/gather | solution.py:71
  191.8 7.0 %fusion.50 = f32[32,128,512]{2,1,0:T(8,128)} fusion(bf16[32,128,512]{2,1,0:T(8,128)(2,1)} %gather_fusion, pred[32]{0:T(512)(128)(4,1)S(1)} %get-tuple-element.124, bf16[128,128,128]{2,1,0:T(8,128)(2,1)} %get-tuple-element.155, s32[]{:T(128)S(6)} %select_n.41, pred[32]{0:T(512)(128)(4,1)S(1)} %get-tuple-element.125), kind=kOutput, calls=%fused_computation.2.clone.1 | convolution fusion | flops 539492352 | bytes 13631556 | tf_op jit(solution)/shard_map/while/body/tpq,tqf->tpf/dot_general | solution.py:72
  198.9 0.1 compare_select_fusion.4
  198.9 18.5 %scatter_fusion = f32[16,128,512]{2,1,0:T(8,128)} fusion(f32[16,128,512]{2,1,0:T(8,128)} %get-tuple-element.139, s32[32]{0:T(128)S(1)} %compare_select_fusion.4, f32[32,128,512]{2,1,0:T(8,128)} %fusion.50), kind=kCustom, calls=%fused_computation.1.clone.1 | custom fusion | flops 2097152 | bytes 25165952 | tf_op jit(solution)/shard_map/while/body/scatter-add | solution.py:75
  217.4 0.7 compare_and_fusion.2
  218.1 6.1 %gather_fusion = bf16[32,128,512]{2,1,0:T(8,128)(2,1)} fusion(bf16[64,128,512]{2,1,0:T(8,128)(2,1)} %get-tuple-element.157, s32[1024]{0:T(1024)S(1)} %pad_clamp_fusion.2), kind=kCustom, calls=%fused_computation.clone.1 | custom fusion | bytes 8388736 | tf_op jit(solution)/shard_map/while/body/jit(_take)/gather | solution.py:71
  224.3 7.0 %fusion.50 = f32[32,128,512]{2,1,0:T(8,128)} fusion(bf16[32,128,512]{2,1,0:T(8,128)(2,1)} %gather_fusion, pred[32]{0:T(512)(128)(4,1)S(1)} %get-tuple-element.124, bf16[128,128,128]{2,1,0:T(8,128)(2,1)} %get-tuple-element.155, s32[]{:T(128)S(6)} %select_n.41, pred[32]{0:T(512)(128)(4,1)S(1)} %get-tuple-element.125), kind=kOutput, calls=%fused_computation.2.clone.1 | convolution fusion | flops 539492352 | bytes 13631556 | tf_op jit(solution)/shard_map/while/body/tpq,tqf->tpf/dot_general | solution.py:72
  231.3 0.1 compare_select_fusion.4
  231.4 18.4 %scatter_fusion = f32[16,128,512]{2,1,0:T(8,128)} fusion(f32[16,128,512]{2,1,0:T(8,128)} %get-tuple-element.139, s32[32]{0:T(128)S(1)} %compare_select_fusion.4, f32[32,128,512]{2,1,0:T(8,128)} %fusion.50), kind=kCustom, calls=%fused_computation.1.clone.1 | custom fusion | flops 2097152 | bytes 25165952 | tf_op jit(solution)/shard_map/while/body/scatter-add | solution.py:75
  249.8 0.0 copy-start.2
  249.8 3.8 %convert_element_type.65 = bf16[16,128,512]{2,1,0:T(8,128)(2,1)} convert(f32[16,128,512]{2,1,0:T(8,128)} %get-tuple-element.48) | non-fusion elementwise | flops 1048576 | bytes 6291456 | tf_op jit(solution)/shard_map/convert_element_type | solution.py:83
  253.7 0.0 reduce-scatter.2.cloned.1.call-update
  253.7 0.0 copy-done
  253.7 0.0 copy-done.2
  253.7 1.6 convolution_add_fusion
  255.3 32.1 %reduce-scatter.2.cloned.1.call-done = bf16[256,512]{1,0:T(8,128)(2,1)} async-done(((bf16[2048,512]{1,0:T(8,128)(2,1)}), bf16[256,512]{1,0:T(8,128)(2,1)}) %reduce-scatter.2.cloned.1.call-update) | async-done | bytes 262160 | tf_op jit(solution)/shard_map/reduce_scatter | solution.py:82
  287.4 1.1 fusion.13
  288.5 0.0 copy-done.3
  288.5 0.0 copy-done.4
  288.5 3.7 %convolution_add_fusion.1 = f32[256,1536]{1,0:T(8,128)} fusion(bf16[512,1536]{1,0:T(8,128)(2,1)} %param.22, bf16[512,512]{1,0:T(8,128)(2,1)} %param.20, f32[1536]{0:T(1024)S(1)} %copy-done.3, bf16[256,512]{1,0:T(8,128)(2,1)} %reduce-scatter.2.cloned.1.call-done, f32[512]{0:T(512)S(1)} %copy-done.4, f32[256]{0:T(256)S(1)} %add_sqrt_fusion), kind=kOutput, calls=%fused_computation.21 | convolution fusion | flops 538050560 | bytes 3941376 | tf_op jit(solution)/shard_map/dot_general | solution.py:18
  292.2 2.8 fusion.18
  (10 shorter events, 0.1 us)
Async XLA Ops:
  6.5 247.1 %copy-start = (bf16[512,1536]{1,0:T(8,128)(2,1)S(1)}, bf16[512,1536]{1,0:T(8,128)(2,1)}, u32[]{:S(2)}) copy-start(bf16[512,1536]{1,0:T(8,128)(2,1)} %param.24) | copy-start | bytes 4718596
  6.5 4.9 %copy-start.1 = (s32[1,1,128]{2,1,0:T(1,128)S(1)}, s32[1,1,128]{2,1,0:T(1,128)}, u32[]{:S(2)}) copy-start(s32[1,1,128]{2,1,0:T(1,128)} %param.18) | copy-start | bytes 1540
  6.5 103.7 %all-gather.3.cloned.1.call-start = ((), (), s32[]{:S(2)}) async-start(), calls=%async_computation.1 | async-start | bytes 8650752 | tf_op jit(solution)/shard_map/all_gather | solution.py:59
  7.3 280.2 %reduce-scatter.2.cloned.1.call-start = ((), (), s32[]{:S(2)}) async-start(), calls=%async_computation.2 | async-start | bytes 2359296 | tf_op jit(solution)/shard_map/reduce_scatter | solution.py:82
  117.9 2.5 copy-start.5
  249.8 3.9 %copy-start.2 = (f32[1536]{0:T(1024)S(1)}, f32[1536]{0:T(1024)}, u32[]{:S(2)}) copy-start(f32[1536]{0:T(1024)} %param.25) | copy-start | bytes 18436
  253.6 34.9 %copy-start.3 = (f32[1536]{0:T(1024)S(1)}, f32[1536]{0:T(1024)}, u32[]{:S(2)}) copy-start(f32[1536]{0:T(1024)} %param.23) | copy-start | bytes 18436
  253.6 34.9 %copy-start.4 = (f32[512]{0:T(512)S(1)}, f32[512]{0:T(512)}, u32[]{:S(2)}) copy-start(f32[512]{0:T(512)} %param.21) | copy-start | bytes 6148
Sparse Core Ops, SparseCore 0:
  10.0 100.2 all-gather.2
  253.8 33.5 reduce-scatter.1
